TPU v7x, 32 devices: a whole 2x2x4 slice. The times are simulated.
32 devices in a mesh: mem: 8 (over z, core), dom: 4 (over y, x).
Axes of the slice: x: 2, y: 2, z: 4, core: 2. Of those that a mesh axis runs over, the one named last changes fastest.
Arguments:
- prior_ensemble: float32 [64, 4, 512, 512], P('mem', None, 'dom'), may hold values from -6 to 6
- spreading_factor: float32 [4], replicated, may hold values from 0.05 to 0.24
- tendency_matrix: float32 [4, 4], replicated, may hold values from -0.6 to 0.6
- measured_data: float32 [4, 4096], P('dom', 'mem'), may hold values from -6 to 6
- inverse_error: float32 [4, 4096], P('dom', 'mem'), may hold values from 0.1 to 1
- assigned_subregion: int32 [4, 4096, 1], P('dom', 'mem'), may hold values from 0 to 31; in each aligned block of 512 rows (0 to 511, 512 to 1023, ..., all dimensions but the last counted through in order) at most 32 rows name the same one
- measured_entry: int32 [4, 4096], P('dom', 'mem'), may hold values from 0 to 8191
- taper_index: int32 [4, 4096], P('dom', 'mem'), may hold values from 0 to 63
- taper_factors: float32 [64], replicated, may hold values from 0.2 to 1
Outputs:
- analysis: float32 [64, 4, 512, 512], P('mem', None, 'dom')
Inputs may be any that keep to these rules, and one draw needn't show every extreme that they name: `assigned_subregion`: in the rows of one device no patch is named by more than 32 rows, a bound that some block reaches.
All inputs are finite; a program needn't handle non-finite values.
Results may differ from a plain program's by a relative error of at most 0.0003.
Values sent between devices are 32-bit elements; how exact they have to be, the bound alone decides.
A program may use at most 128 MiB of HBM per device.

v0:
```python
import jax
import jax.numpy as jnp
from jax import lax
from jax.sharding import PartitionSpec as P

PATCH = 2048
NS_ITERS = 5


HIGH = lax.Precision.HIGHEST


def padded(block, sides, width):
    for axis, dim in sides:
        count = lax.axis_size(axis)
        forward = [(i, i + 1) for i in range(count - 1)]
        backward = [(target, source) for source, target in forward]
        low = lax.ppermute(
            lax.slice_in_dim(block, block.shape[dim] - width, None, axis=dim), axis, forward
        )
        high = lax.ppermute(lax.slice_in_dim(block, 0, width, axis=dim), axis, backward)
        block = jnp.concatenate([low, block, high], axis=dim)
    return block


def laplacian_update(haloed_ensemble, ensemble, spreading_factor, tendency_matrix):
    subdomain_lines = ensemble.shape[2]
    beside = jnp.pad(ensemble, ((0, 0), (0, 0), (0, 0), (1, 1)))
    laplace = (
        haloed_ensemble[:, :, 2:]
        + haloed_ensemble[:, :, :subdomain_lines]
        + beside[:, :, :, 2:]
        + beside[:, :, :, :-2]
        - 4.0 * ensemble
    )
    mixing = jnp.einsum("vw,kwxy->kvxy", tendency_matrix, ensemble, precision=HIGH)
    return ensemble + spreading_factor[None, :, None, None] * laplace + mixing


def transforms(gram, drive, member_count):
    identity_m = jnp.eye(member_count, dtype=jnp.float32)
    system = (member_count - 1.0) * identity_m + gram
    norm_value = jnp.sqrt(jnp.sum(system * system, axis=(-2, -1)))
    iterate = system / norm_value[..., None, None]
    inverse = jnp.broadcast_to(identity_m, system.shape)
    for sweep_no in range(NS_ITERS):
        middle = 1.5 * identity_m - 0.5 * jnp.einsum(
            "...ij,...jk->...ik", inverse, iterate, precision=HIGH
        )
        iterate = jnp.einsum("...ij,...jk->...ik", iterate, middle, precision=HIGH)
        inverse = jnp.einsum("...ij,...jk->...ik", middle, inverse, precision=HIGH)
    root = inverse / jnp.sqrt(norm_value)[..., None, None]
    inner = jnp.einsum("...ij,...j->...i", root, drive, precision=HIGH)
    offset = jnp.einsum("...ij,...j->...i", root, inner, precision=HIGH)
    return offset[..., :, None] + jnp.sqrt(member_count - 1.0) * root


def slot_ranks(patch_ids, patch_count):
    onehot = (patch_ids[..., None] == jnp.arange(patch_count, dtype=jnp.int32)).astype(jnp.int32)
    before = jnp.cumsum(onehot, axis=-2) - onehot
    return jnp.sum(before * onehot, axis=-1)


def shards(
    prior_ensemble,
    spreading_factor,
    tendency_matrix,
    measured_data,
    inverse_error,
    assigned_subregion,
    measured_entry,
    taper_index,
    taper_factors,
):
    ensemble_share, prognostic_number, subdomain_lines, eastward_span = prior_ensemble.shape
    groups = lax.axis_size("mem")
    members = ensemble_share * groups
    cells_dev = subdomain_lines * eastward_span // groups
    per_device = cells_dev // PATCH
    per_tile = per_device * groups
    haloed_ensemble = padded(prior_ensemble, (("dom", 2),), 1)
    advanced_ensemble = laplacian_update(
        haloed_ensemble, prior_ensemble, spreading_factor, tendency_matrix
    )
    moved = lax.all_to_all(
        advanced_ensemble.reshape(ensemble_share, prognostic_number, groups, cells_dev),
        "mem",
        split_axis=2,
        concat_axis=0,
        tiled=True,
    )
    ensemble = moved.reshape(members, prognostic_number, cells_dev)
    patch_ids = assigned_subregion.reshape(-1)
    obs_rows = patch_ids.shape[0]
    capacity = 2 * obs_rows // per_tile
    table_levels = taper_factors.shape[0]
    picks = (
        taper_index.reshape(-1)[:, None] == jnp.arange(table_levels, dtype=jnp.int32)[None, :]
    ).astype(jnp.float32)
    weight = inverse_error.reshape(-1) * jnp.dot(picks, taper_factors, precision=HIGH)
    values = measured_data.reshape(-1)
    columns = measured_entry.reshape(-1).astype(jnp.float32)
    target = patch_ids * capacity + slot_ranks(patch_ids, per_tile)

    def place_rows(field):
        return (
            jnp.zeros((per_tile * capacity,), jnp.float32)
            .at[target]
            .set(field)
            .reshape(groups, per_device * capacity)
        )

    received = (
        lax.all_to_all(place_rows(values), "mem", split_axis=0, concat_axis=0, tiled=True),
        lax.all_to_all(place_rows(weight), "mem", split_axis=0, concat_axis=0, tiled=True),
        lax.all_to_all(place_rows(columns), "mem", split_axis=0, concat_axis=0, tiled=True),
    )

    def arrange(field):
        return (
            field.reshape(groups, per_device, capacity)
            .transpose(1, 0, 2)
            .reshape(per_device, groups * capacity)
        )

    slot_value = arrange(received[0])
    slot_weight = arrange(received[1])
    slot_column = arrange(received[2])
    centre = jnp.mean(ensemble, axis=0)
    deviation = ensemble - centre[None]
    column_ids = slot_column.astype(jnp.int32)
    flat_index = (
        column_ids // PATCH * cells_dev
        + jnp.arange(per_device, dtype=jnp.int32)[:, None] * PATCH
        + column_ids % PATCH
    )
    flat_index = flat_index.reshape(-1)
    flat_dev = deviation.reshape(members, prognostic_number * cells_dev)
    obs_dev = jnp.take(flat_dev, flat_index, axis=1).reshape(members, per_device, -1)
    innovation = slot_value - jnp.take(centre.reshape(-1), flat_index).reshape(per_device, -1)
    weighted = obs_dev * slot_weight[None]
    gram = jnp.einsum("kps,jps->pkj", weighted, obs_dev, precision=HIGH)
    drive = jnp.einsum("kps,ps->pk", weighted, innovation, precision=HIGH)
    coeffs = transforms(gram, drive, members)
    dev_blocks = deviation.reshape(members, prognostic_number, per_device, PATCH)
    mixed = jnp.einsum("pjk,jvpt->kvpt", coeffs, dev_blocks, precision=HIGH)
    analysed = centre.reshape(1, prognostic_number, per_device, PATCH) + mixed
    outgoing = analysed.reshape(groups, ensemble_share, prognostic_number, cells_dev)
    returned = lax.all_to_all(outgoing, "mem", split_axis=0, concat_axis=3, tiled=True)
    return returned.reshape(ensemble_share, prognostic_number, subdomain_lines, eastward_span)


def solution(mesh):
    in_specs = (
        P("mem", None, "dom", None),
        P(),
        P(),
        P("dom", "mem"),
        P("dom", "mem"),
        P("dom", "mem", None),
        P("dom", "mem"),
        P("dom", "mem"),
        P(),
    )
    out_specs = P("mem", None, "dom", None)
    return jax.shard_map(shards, mesh=mesh, in_specs=in_specs, out_specs=out_specs, check_vma=False)
```

profile of v0, /device:TPU:0, one launch (start us, length us, event | category | flops | bytes accessed | tf_op | source)
XLA Modules:
  0.0 609.6 jit_solution(14362782641976846216)
XLA Ops:
  0.0 0.7 fusion.39
  0.7 1.2 reduce-window.6
  2.1 0.8 fusion.33
  2.9 0.7 compare_select_fusion.1
  3.6 0.7 convert_element_type.53
  4.3 3.0 scatter_custom_fusion
  7.3 6.4 %all-to-all-start.1 = ((f32[8,1,128]{2,1,0:T(1,128)}), f32[8,1,128]{2,1,0:T(1,128)S(1)}, u32[]{:S(2)}, u32[]{:S(2)}) async-start(f32[8,1,128]{2,1,0:T(1,128)} %bitcast.14), calls=%async_computation.1 | async-start | bytes 8192 | tf_op jit(solution)/shard_map/all_to_all | solution.py:116
  13.6 1.3 fusion.63
  15.0 1.3 collective-permute-start
  16.3 4.7 collective-permute-start.1
  21.0 25.0 %fusion.8 = f32[8,128,512,4]{2,3,1,0:T(4,128)} fusion(f32[8,4,128,512]{3,2,1,0:T(8,128)} %param.9, f32[4,4]{1,0:T(4,128)S(1)} %copy-done), kind=kOutput, calls=%fused_computation.19 | convolution fusion | flops 100663296 | bytes 16777280 | tf_op jit(solution)/shard_map/vw,kwxy->kvxy/dot_general | solution.py:36
  46.0 3.2 scatter_custom_fusion.2
  49.1 5.1 all-to-all-start.3
  54.3 0.3 fusion.18
  54.6 3.0 scatter_custom_fusion.1
  57.6 2.2 all-to-all-done.3
  59.8 3.2 all-to-all-start.2
  63.1 22.8 %fusion.5 = f32[8,4,128,512]{3,2,1,0:T(8,128)} fusion(f32[8,4,128,512]{3,2,1,0:T(8,128)} %param.9, f32[8,4,1,512]{3,2,1,0:T(1,128)S(1)} %collective-permute-done.1, f32[8,4,1,512]{3,2,1,0:T(1,128)S(1)} %collective-permute-done, f32[8,128,512,4]{2,3,1,0:T(4,128)} %fusion.8, f32[4]{0:T(128)S(1)} %copy-done.3), kind=kLoop, calls=%fused_computation.12 | loop fusion | flops 20971520 | bytes 25296912 | tf_op jit(solution)/shard_map/add | solution.py:37
  85.9 9.4 %reshape.273 = f32[8,4,8,8192]{3,2,1,0:T(8,128)} reshape(f32[8,4,128,512]{3,2,1,0:T(8,128)} %fusion.5) | data formatting | bytes 16777216 | tf_op jit(solution)/shard_map/reshape | solution.py:86
  95.3 12.0 %copy.84 = f32[8,4,8,8192]{3,1,0,2:T(4,128)} copy(f32[8,4,8,8192]{3,2,1,0:T(8,128)} %reshape.273) | data formatting | bytes 16777216 | tf_op jit(solution)/shard_map/reshape | solution.py:86
  107.3 5.3 all-to-all-start
  113.0 0.5 broadcast.335
  113.5 0.7 reduce.14
  114.3 0.7 reduce.13
  115.2 181.3 %all-to-all-done = f32[8,4,8,8192]{3,1,0,2:T(4,128)} async-done(((f32[8,4,8,8192]{3,1,0,2:T(4,128)}), f32[8,4,8,8192]{3,1,0,2:T(4,128)}, u32[]{:S(2)}, u32[]{:S(2)}) %all-to-all-start) | async-done | bytes 8388640 | tf_op jit(solution)/shard_map/all_to_all | solution.py:85
  296.5 4.2 bitcast_reduce_fusion
  300.7 6.2 %gather_fusion.1 = f32[1024]{0:T(1024)S(1)} fusion(f32[32768]{0:T(1024)S(1)} %bitcast.131, s32[1024]{0:T(1024)S(1)} %broadcast_clamp_fusion), kind=kCustom, calls=%fused_computation.1 | custom fusion | bytes 12288 | tf_op jit(solution)/shard_map/jit(_take)/gather | solution.py:140
  306.9 8.1 %copy.111 = f32[8,8,4,8192]{3,1,2,0:T(8,128)S(1)} copy(f32[8,8,4,8192]{3,2,1,0:T(4,128)} %bitcast.56) | data formatting | bytes 16777216
  315.1 4.0 broadcast_subtract_fusion
  319.1 12.2 %copy.90 = f32[64,32768]{0,1:T(8,128)} copy(f32[64,32768]{1,0:T(8,128)} %broadcast_subtract_fusion) | data formatting | bytes 16777216 | tf_op jit(solution)/shard_map/sub | solution.py:130
  331.3 8.6 %gather_fusion = f32[1024,64]{1,0:T(8,128)S(1)} fusion(f32[64,32768]{0,1:T(8,128)} %copy.90, s32[1024]{0:T(1024)S(1)} %broadcast_clamp_fusion), kind=kCustom, calls=%fused_computation | custom fusion | bytes 528384 | tf_op jit(solution)/shard_map/jit(_take)/gather | solution.py:139
  340.2 0.5 multiply_reduce_fusion
  340.7 0.3 fusion.15
  341.0 0.3 fusion.43
  342.4 0.3 fusion.13
  343.2 0.3 fusion.12
  344.0 0.3 convolution_bitcast_fusion.1
  344.3 0.3 fusion.11
  344.9 0.3 convolution_bitcast_fusion
  345.2 0.3 fusion.70
  345.5 12.1 %reshape.334 = f32[64,4,4,2048]{3,2,1,0:T(4,128)} reshape(f32[8,8,4,1,8192]{4,2,1,0,3:T(4,128)} %bitcast.4) | data formatting | bytes 16777216 | tf_op jit(solution)/shard_map/reshape | solution.py:92
  357.6 20.7 %bitcast_add_fusion = f32[64,4,4,2048]{3,0,1,2:T(8,128)} fusion(f32[64,4,4,2048]{3,2,1,0:T(4,128)} %reshape.334, f32[4,4,2048]{2,0,1:T(4,128)S(1)} %bitcast.136, f32[4,64,64]{2,1,0:T(8,128)S(1)} %convolution_divide_fusion, f32[4,64]{1,0:T(4,128)S(1)} %bitcast.140), kind=kOutput, calls=%fused_computation.16 | convolution fusion | flops 1614839808 | bytes 16974848 | tf_op jit(solution)/shard_map/pjk,jvpt->kvpt/dot_general | solution.py:146
  378.3 12.2 %copy.95 = f32[64,4,4,2048]{3,2,0,1:T(4,128)} copy(f32[64,4,4,2048]{3,0,1,2:T(8,128)} %bitcast_add_fusion) | data formatting | bytes 16777216 | tf_op jit(solution)/shard_map/add | solution.py:147
  390.5 10.9 %reshape.282 = f32[8,8,4,8192]{3,1,0,2:T(8,128)} reshape(f32[64,4,4,2048]{3,2,0,1:T(4,128)} %copy.95) | data formatting | bytes 16777216 | tf_op jit(solution)/shard_map/reshape | solution.py:148
  401.3 3.9 copy.96
  405.3 186.6 %all_to_all.57 = f32[8,8,4,8192]{3,1,2,0:T(8,128)S(1)} all-to-all(f32[8,8,4,8192]{3,1,2,0:T(8,128)S(1)} %copy.96), channel_id=1, replica_groups=mesh['mem'=8,'dom'=4] {'mem'}, dimensions={0} | all-to-all | bytes 16777216 | tf_op jit(solution)/shard_map/all_to_all | solution.py:149
  591.9 8.1 %copy.97 = f32[1,8,4,8,8192]{4,3,2,1,0:T(8,128)} copy(f32[1,8,4,8,8192]{4,1,2,3,0:T(8,128)S(1)} %bitcast.134) | data formatting | bytes 16777216 | tf_op jit(solution)/shard_map/all_to_all | solution.py:149
  600.0 9.4 %reshape.283 = f32[8,4,128,512]{3,2,1,0:T(8,128)} reshape(f32[1,8,4,8,8192]{4,3,2,1,0:T(8,128)} %copy.97) | data formatting | bytes 16777216 | tf_op jit(solution)/shard_map/reshape | solution.py:150
  (54 shorter events, 3.7 us)
Async XLA Ops:
  0.0 21.0 %copy-start = (f32[4,4]{1,0:T(4,128)S(1)}, f32[4,4]{1,0:T(4,128)}, u32[]{:S(2)}) copy-start(f32[4,4]{1,0:T(4,128)} %param.11) | copy-start | bytes 196
  7.3 41.9 %all-to-all-start.1 = ((f32[8,1,128]{2,1,0:T(1,128)}), f32[8,1,128]{2,1,0:T(1,128)S(1)}, u32[]{:S(2)}, u32[]{:S(2)}) async-start(f32[8,1,128]{2,1,0:T(1,128)} %bitcast.14), calls=%async_computation.1 | async-start | bytes 8192 | tf_op jit(solution)/shard_map/all_to_all | solution.py:116
  15.0 48.1 %collective-permute-start = (f32[8,4,1,512]{3,2,1,0:T(1,128)S(1)}, f32[8,4,1,512]{3,2,1,0:T(1,128)S(1)}, u32[]{:S(2)}, u32[]{:S(2)}) collective-permute-start(f32[8,4,1,512]{3,2,1,0:T(1,128)S(1)} %get-tuple-element.7), channel_id=1, source_target_pairs={{1,0},{2,1},{3,2},{5,4},{6,5},{7,6},{9,8},{10,9},{11,10},{13,12},{... | collective-permute-start | bytes 196616 | tf_op jit(solution)/shard_map/ppermute | solution.py:21
  16.3 38.0 %copy-start.4 = (s32[1,512]{1,0:T(1,128)S(1)}, s32[1,512]{1,0:T(1,128)}, u32[]{:S(2)}) copy-start(s32[1,512]{1,0:T(1,128)} %param.16) | copy-start | bytes 6148
  16.3 38.0 %copy-start.5 = (f32[64]{0:T(128)S(1)}, f32[64]{0:T(128)}, u32[]{:S(2)}) copy-start(f32[64]{0:T(128)} %param.17) | copy-start | bytes 772
  16.3 38.3 %copy-start.2 = (f32[1,512]{1,0:T(1,128)S(1)}, f32[1,512]{1,0:T(1,128)}, u32[]{:S(2)}) copy-start(f32[1,512]{1,0:T(1,128)} %param.13) | copy-start | bytes 6148
  16.3 46.8 %copy-start.3 = (f32[4]{0:T(128)S(1)}, f32[4]{0:T(128)}, u32[]{:S(2)}) copy-start(f32[4]{0:T(128)} %param.10) | copy-start | bytes 52
  16.3 46.8 %collective-permute-start.1 = (f32[8,4,1,512]{3,2,1,0:T(1,128)S(1)}, f32[8,4,1,512]{3,2,1,0:T(1,128)S(1)}, u32[]{:S(2)}, u32[]{:S(2)}) collective-permute-start(f32[8,4,1,512]{3,2,1,0:T(1,128)S(1)} %get-tuple-element.8), channel_id=1, source_target_pairs={{0,1},{1,2},{2,3},{4,5},{5,6},{6,7},{8,9},{9,10},{10,11},{12,13},{... | collective-permute-start | bytes 196616 | tf_op jit(solution)/shard_map/ppermute | solution.py:18
  49.1 10.7 %all-to-all-start.3 = ((f32[8,1,128]{2,1,0:T(1,128)}), f32[8,1,128]{2,1,0:T(1,128)S(1)}, u32[]{:S(2)}, u32[]{:S(2)}) async-start(f32[8,1,128]{2,1,0:T(1,128)} %bitcast.26), calls=%async_computation.3 | async-start | bytes 8192 | tf_op jit(solution)/shard_map/all_to_all | solution.py:114
  59.8 47.5 %all-to-all-start.2 = ((f32[8,1,128]{2,1,0:T(1,128)}), f32[8,1,128]{2,1,0:T(1,128)S(1)}, u32[]{:S(2)}, u32[]{:S(2)}) async-start(f32[8,1,128]{2,1,0:T(1,128)} %bitcast.23), calls=%async_computation.2 | async-start | bytes 8192 | tf_op jit(solution)/shard_map/all_to_all | solution.py:115
  107.3 189.2 %all-to-all-start = ((f32[8,4,8,8192]{3,1,0,2:T(4,128)}), f32[8,4,8,8192]{3,1,0,2:T(4,128)}, u32[]{:S(2)}, u32[]{:S(2)}) async-start(f32[8,4,8,8192]{3,1,0,2:T(4,128)} %copy.84), calls=%async_computation | async-start | bytes 16777216 | tf_op jit(solution)/shard_map/all_to_all | solution.py:85
  591.9 17.4 %copy-start.1 = (f32[4,4]{1,0:T(4,128)S(1)}, f32[4,4]{1,0:T(4,128)}, u32[]{:S(2)}) copy-start(f32[4,4]{1,0:T(4,128)} %param.11) | copy-start | bytes 196
where the time goes:
time: 621 us; the launch traced here: 610 us
  blocking collectives  187 us (30%)
  waiting for transfers between devices  183 us (29%)
  local copies, waits for them, and re-layouts  125 us (20%)
  matrix products  51.1 us (8%)
  other arithmetic  36.7 us (6%)
  starting transfers between devices  25.9 us (4%)
    all_to_all x1, blocking collectives, shards(): lax.all_to_all(outgoing, 'mem', split_axis=0, concat_axis=3, tiled=True)  187 us
    all_to_all x1, waiting for transfers between devices, shards(): lax.all_to_all(advanced_ensemble.reshape(ensemble_share, prognostic_numbe...  181 us
    dot_general x1, matrix products, laplacian_update(): jnp.einsum('vw,kwxy->kvxy', tendency_matrix, ensemble, precision=HIGH)  25 us
    add x1, other arithmetic, laplacian_update(): return ensemble + spreading_factor[None, :, None, None] * laplace + mixing  22.8 us
    reshape x2, local copies, waits for them, and re-layouts, shards(): advanced_ensemble.reshape(ensemble_share, prognostic_number, groups, cell...  21.3 us
    dot_general x1, matrix products, shards(): mixed = jnp.einsum('pjk,jvpt->kvpt', coeffs, dev_blocks, precision=HIGH)  20.7 us
    reshape x2, local copies, waits for them, and re-layouts, shards(): analysed.reshape(groups, ensemble_share, prognostic_number, cells_dev)  14.8 us
  transfers between devices with their start and end apart: 6, of which 2 were waited for; matrix products, arithmetic and copies ran while one was open for 13% of the time, Pallas kernels for 0%

commit v1 on v0

--- a/solution.py
+++ b/solution.py
@@ -1,6 +1,10 @@
+import functools
+
 import jax
 import jax.numpy as jnp
 from jax import lax
+from jax.experimental import pallas as pl
+from jax.experimental.pallas import tpu as pltpu
 from jax.sharding import PartitionSpec as P
 
 PATCH = 2048
@@ -150,6 +154,320 @@
     return returned.reshape(ensemble_share, prognostic_number, subdomain_lines, eastward_span)
 
 
+LANES = 128
+
+
+def split3(field):
+    high = field.astype(jnp.bfloat16)
+    rest = field - high.astype(jnp.float32)
+    middle = rest.astype(jnp.bfloat16)
+    low = (rest - middle.astype(jnp.float32)).astype(jnp.bfloat16)
+    return [high, middle, low]
+
+
+def dot(a, b, dims=((1,), (0,))):
+    return lax.dot_general(
+        a, b, (dims, ((), ())), precision=HIGH, preferred_element_type=jnp.float32
+    )
+
+
+def analysis_kernel(
+    groups, tiles, per_device, patch_lines, lanes_own,
+    factor, tendency, state, obs, result,
+    field, outbox, inbox, answer, obs_in, dev, centre, picked,
+    load_sem, halo_send, halo_recv, obs_send, obs_recv, obs_own,
+    go_send, go_recv, go_own, back_send, back_recv, back_own,
+):
+    mine = lax.axis_index("mem")
+    tile = lax.axis_index("dom")
+    variables, lines, share, span = state.shape
+    members = groups * share
+    device_lines = per_device * patch_lines
+    chunks = variables * patch_lines
+    order = sorted(range(1, groups), key=lambda t: abs(t - groups // 2))
+    upper = lax.rem(tile + 1, tiles)
+    lower = lax.rem(tile + tiles - 1, tiles)
+
+    load = pltpu.make_async_copy(state, field.at[:, pl.ds(1, lines)], load_sem)
+    load.start()
+
+    barrier = pltpu.get_barrier_semaphore()
+    for t in range(1, groups):
+        pl.semaphore_signal(barrier, 1, device_id={"mem": lax.rem(mine + t, groups)})
+    for other in (upper, lower):
+        pl.semaphore_signal(barrier, 1, device_id={"dom": other})
+    pl.semaphore_wait(barrier, groups + 1)
+
+    halos = []
+    for side, (line, place, other) in enumerate(((lines - 1, 0, upper), (0, lines + 1, lower))):
+        halos.append(
+            pltpu.make_async_remote_copy(
+                src_ref=state.at[:, pl.ds(line, 1)],
+                dst_ref=field.at[:, pl.ds(place, 1)],
+                send_sem=halo_send.at[side],
+                recv_sem=halo_recv.at[side],
+                device_id={"dom": other},
+            )
+        )
+        halos[-1].start()
+
+    def obs_copy(t):
+        to = lax.rem(mine + t, groups)
+        return pltpu.make_async_remote_copy(
+            src_ref=obs.at[to],
+            dst_ref=obs_in.at[mine],
+            send_sem=obs_send.at[t],
+            recv_sem=obs_recv.at[t],
+            device_id={"mem": to},
+        )
+
+    def go_copy(p, t):
+        to = lax.rem(mine + t, groups)
+        return pltpu.make_async_remote_copy(
+            src_ref=outbox.at[to, p],
+            dst_ref=inbox.at[p, mine],
+            send_sem=go_send.at[p, t],
+            recv_sem=go_recv.at[p, t],
+            device_id={"mem": to},
+        )
+
+    def go_local(p):
+        return pltpu.make_async_copy(outbox.at[mine, p], inbox.at[p, mine], go_own.at[p])
+
+    def result_lines(p):
+        return result.at[:, pl.ds(mine * device_lines + p * patch_lines, patch_lines)]
+
+    def back_copy(p, t):
+        to = lax.rem(mine + t, groups)
+        return pltpu.make_async_remote_copy(
+            src_ref=answer.at[p, to],
+            dst_ref=result_lines(p),
+            send_sem=back_send.at[p, t],
+            recv_sem=back_recv.at[p, t],
+            device_id={"mem": to},
+        )
+
+    def back_local(p):
+        return pltpu.make_async_copy(answer.at[p, mine], result_lines(p), back_own.at[p])
+
+    for t in range(1, groups):
+        obs_copy(t).start()
+    keep = pltpu.make_async_copy(obs.at[mine], obs_in.at[mine], obs_own)
+    keep.start()
+
+    load.wait()
+    for copy in halos:
+        copy.wait()
+    for place, outside in ((0, tile == 0), (lines + 1, tile == tiles - 1)):
+        for v in range(variables):
+            field[v, place] = jnp.where(outside, 0.0, field[v, place])
+
+    lane = lax.broadcasted_iota(jnp.int32, (share, span), 1)
+
+    def advance(p, to):
+        def one_line(r, carry):
+            line = to * device_lines + p * patch_lines + r
+            here = [field[w, line + 1] for w in range(variables)]
+            for v in range(variables):
+                own = here[v]
+                west = jnp.where(lane == 0, 0.0, pltpu.roll(own, 1, 1))
+                east = jnp.where(lane == span - 1, 0.0, pltpu.roll(own, span - 1, 1))
+                laplace = field[v, line + 2] + field[v, line] + east + west - 4.0 * own
+                total = own + factor[v] * laplace
+                for w in range(variables):
+                    total += tendency[v, w] * here[w]
+                outbox[to, p, v, r] = total
+            return carry
+
+        lax.fori_loop(0, patch_lines, one_line, 0)
+
+    def forecast(p, carry):
+        for t in order:
+            advance(p, lax.rem(mine + t, groups))
+            go_copy(p, t).start()
+        advance(p, mine)
+        go_local(p).start()
+        return carry
+
+    lax.fori_loop(0, per_device, forecast, 0)
+
+    for t in range(1, groups):
+        obs_copy(t).wait()
+    keep.wait()
+
+    slots = -(-groups // lanes_own) * LANES
+    rows_i = lax.broadcasted_iota(jnp.int32, (members, members), 0)
+    cols_i = lax.broadcasted_iota(jnp.int32, (members, members), 1)
+    identity = jnp.where(rows_i == cols_i, 1.0, 0.0)
+    cell = lax.broadcasted_iota(jnp.int32, (span, slots), 0)
+
+    def analyse(p, carry):
+        packs = []
+        for first in range(0, groups, lanes_own):
+            pack = obs_in[first, p]
+            for s in range(first + 1, min(first + lanes_own, groups)):
+                pack += obs_in[s, p]
+            packs.append(pack)
+        pack = jnp.concatenate(packs, axis=1)
+        value, weight = pack[0:1], pack[1:2]
+        column = pack[2:3].astype(jnp.int32)
+        picked[...] = jnp.zeros_like(picked)
+        for t in range(1, groups):
+            go_copy(p, t).wait_recv()
+        go_local(p).wait()
+
+        def gather(c, carry):
+            v, r = c // patch_lines, c % patch_lines
+            block = inbox[p, :, v, r].reshape(members, span)
+            mean = jnp.sum(block, axis=0, keepdims=True) * (1.0 / members)
+            away = block - mean
+            dev[c] = away
+            wide = jnp.broadcast_to(mean, (16, span))
+            centre[c] = wide[:8]
+            parts = jnp.concatenate(split3(away) + split3(wide), axis=0)
+            chosen = jnp.where(cell == column - c * span, 1.0, 0.0).astype(jnp.bfloat16)
+            picked[...] += jnp.dot(parts, chosen, preferred_element_type=jnp.float32)
+            return carry
+
+        lax.fori_loop(0, chunks, gather, 0)
+        seen = picked[0:members] + picked[members : 2 * members] + picked[2 * members : 3 * members]
+        low = 3 * members
+        middle_seen = picked[low : low + 8] + picked[low + 16 : low + 24] + picked[low + 32 : low + 40]
+        innovation = value - middle_seen
+        weighted = seen * weight
+        gram = dot(weighted, seen, ((1,), (1,)))
+        drive = jnp.sum(weighted * innovation[0:1], axis=1, keepdims=True)
+        system = (members - 1.0) * identity + gram
+        squares = jnp.sum(system * system, axis=1, keepdims=True)
+        norm = jnp.sqrt(jnp.sum(squares, axis=0, keepdims=True))
+
+        def sweep(i, pair):
+            middle = 1.5 * identity - 0.5 * dot(pair[:, members:], pair[:, :members])
+            return dot(middle, pair)
+
+        start = jnp.concatenate([system / norm, identity], axis=1)
+        pair = start
+        for i in range(NS_ITERS):
+            pair = sweep(i, pair)
+        inverse = pair[:, members:]
+        root = inverse / jnp.sqrt(norm)
+        inner = jnp.sum(root * drive, axis=0, keepdims=True)
+        offset = jnp.sum(root * inner, axis=1, keepdims=True)
+        offset = jnp.sum(identity * offset, axis=0, keepdims=True)
+        coeffs = offset + float(members - 1) ** 0.5 * root
+
+        def mix(c, carry):
+            v, r = c // patch_lines, c % patch_lines
+            mixed = dot(coeffs, dev[c]) + centre[c, 0:1]
+            answer[p, :, v, r] = mixed.reshape(groups, share, span)
+            return carry
+
+        lax.fori_loop(0, chunks, mix, 0)
+        for t in order:
+            back_copy(p, t).start()
+        back_local(p).start()
+        return carry
+
+    lax.fori_loop(0, per_device, analyse, 0)
+
+    def finish(p, carry):
+        for t in range(1, groups):
+            go_copy(p, t).wait_send()
+        for t in range(1, groups):
+            back_copy(p, t).wait()
+        back_local(p).wait()
+        return carry
+
+    lax.fori_loop(0, per_device, finish, 0)
+
+
+def fused(
+    prior_ensemble,
+    spreading_factor,
+    tendency_matrix,
+    measured_data,
+    inverse_error,
+    assigned_subregion,
+    measured_entry,
+    taper_index,
+    taper_factors,
+):
+    share, variables, lines, span = prior_ensemble.shape
+    groups, tiles = lax.axis_size("mem"), lax.axis_size("dom")
+    patch_lines = PATCH // span
+    per_device = lines // groups // patch_lines
+    per_tile = per_device * groups
+    members = share * groups
+    patch_ids = assigned_subregion.reshape(-1)
+    obs_rows = patch_ids.shape[0]
+    capacity = 2 * obs_rows // per_tile
+    lanes_own = LANES // capacity
+    levels = jnp.arange(taper_factors.shape[0], dtype=jnp.int32)
+    taper = jnp.sum(
+        jnp.where(taper_index.reshape(-1)[:, None] == levels[None], taper_factors[None], 0.0), axis=1
+    )
+    weight = inverse_error.reshape(-1) * taper
+    number = jnp.arange(obs_rows, dtype=jnp.int32)
+    rank = jnp.sum(
+        ((patch_ids[None, :] == patch_ids[:, None]) & (number[None, :] < number[:, None])).astype(jnp.int32),
+        axis=1,
+    )
+    slot = lax.rem(lax.axis_index("mem"), lanes_own) * capacity + rank
+    nothing = jnp.zeros_like(weight)
+    fields = jnp.stack(
+        [measured_data.reshape(-1), weight, measured_entry.reshape(-1).astype(jnp.float32)]
+        + [nothing] * 5
+    )
+    patches = jnp.arange(per_tile, dtype=jnp.int32)
+    spread = jnp.where(patch_ids[None, None] == patches[:, None, None], fields[None], 0.0)
+    places = (slot[:, None] == jnp.arange(LANES, dtype=jnp.int32)[None]).astype(jnp.float32)
+    obs = jnp.dot(spread.reshape(per_tile * 8, obs_rows), places, precision=HIGH)
+    obs = obs.reshape(groups, per_device, 8, LANES)
+    state = prior_ensemble.transpose(1, 2, 0, 3)
+    chunks = variables * patch_lines
+    slots = -(-groups // lanes_own) * LANES
+    dma = pltpu.SemaphoreType.DMA
+    result = pl.pallas_call(
+        functools.partial(analysis_kernel, groups, tiles, per_device, patch_lines, lanes_own),
+        out_shape=jax.ShapeDtypeStruct(state.shape, jnp.float32),
+        in_specs=[
+            pl.BlockSpec(memory_space=pltpu.SMEM),
+            pl.BlockSpec(memory_space=pltpu.SMEM),
+            pl.BlockSpec(memory_space=pl.ANY),
+            pl.BlockSpec(memory_space=pltpu.VMEM),
+        ],
+        out_specs=pl.BlockSpec(memory_space=pl.ANY),
+        scratch_shapes=[
+            pltpu.VMEM((variables, lines + 2, share, span), jnp.float32),
+            pltpu.VMEM((groups, per_device, variables, patch_lines, share, span), jnp.float32),
+            pltpu.VMEM((per_device, groups, variables, patch_lines, share, span), jnp.float32),
+            pltpu.VMEM((per_device, groups, variables, patch_lines, share, span), jnp.float32),
+            pltpu.VMEM((groups, per_device, 8, LANES), jnp.float32),
+            pltpu.VMEM((chunks, members, span), jnp.float32),
+            pltpu.VMEM((chunks, 8, span), jnp.float32),
+            pltpu.VMEM((3 * members + 48, slots), jnp.float32),
+            dma, dma((2,)), dma((2,)), dma((groups,)), dma((groups,)), dma,
+            dma((per_device, groups)), dma((per_device, groups)), dma((per_device,)),
+            dma((per_device, groups)), dma((per_device, groups)), dma((per_device,)),
+        ],
+        compiler_params=pltpu.CompilerParams(
+            collective_id=0, has_side_effects=True, vmem_limit_bytes=60 * 1024 * 1024
+        ),
+    )(spreading_factor, tendency_matrix, state, obs)
+    return result.transpose(2, 0, 1, 3)
+
+
+def step(prior_ensemble, *rest):
+    share, _, lines, span = prior_ensemble.shape
+    groups, tiles = lax.axis_size("mem"), lax.axis_size("dom")
+    whole_lines = PATCH % span == 0 and lines % (groups * (PATCH // span)) == 0
+    obs_rows = rest[2].shape[-1]
+    capacity = 2 * obs_rows * PATCH // (lines * span)
+    if share % 8 == 0 and whole_lines and tiles > 1 and groups > 1 and LANES % capacity == 0:
+        return fused(prior_ensemble, *rest)
+    return shards(prior_ensemble, *rest)
+
+
 def solution(mesh):
     in_specs = (
         P("mem", None, "dom", None),
@@ -163,4 +481,4 @@
         P(),
     )
     out_specs = P("mem", None, "dom", None)
-    return jax.shard_map(shards, mesh=mesh, in_specs=in_specs, out_specs=out_specs, check_vma=False)
+    return jax.shard_map(step, mesh=mesh, in_specs=in_specs, out_specs=out_specs, check_vma=False)

time: 621 us -> 401 us (0.65)
  the two profiles are of different devices: /device:TPU:0 before, /device:TPU:9 now
where the time goes in v1:
time: 401 us
  Pallas kernels  372 us (93%)
  local copies, waits for them, and re-layouts  24 us (6%)
    pallas_call x1, Pallas kernels, fused(): pl.pallas_call(functools.partial(analysis_kernel, groups, tiles, per_devi...  372 us
    transpose x1, local copies, waits for them, and re-layouts, fused(): return result.transpose(2, 0, 1, 3)  11.6 us
    unnamed x1, local copies, waits for them, and re-layouts  11.6 us

profile of v1, /device:TPU:9, one launch (start us, length us, event | category | flops | bytes accessed | tf_op | source)
XLA Modules:
  0.0 400.7 jit_solution(325624806884097958)
XLA Ops:
  0.0 1.0 convert_reduce_fusion
  1.0 0.7 convert_element_type.8
  1.7 0.8 select_reduce_fusion
  2.5 0.7 mul.7
  3.2 0.7 stack.9
  3.9 0.8 broadcast_compare_fusion
  4.7 1.2 fusion.1.obs
  5.8 11.6 %copy.16 = f32[8,4,128,512]{3,0,2,1:T(8,128)} copy(f32[8,4,128,512]{3,2,1,0:T(8,128)} %param.9) | data formatting | bytes 16777216 | tf_op args[0]
  17.5 371.6 %shard_map.91 = f32[4,128,8,512]{3,2,1,0:T(8,128)} custom-call(f32[4]{0:T(128)} %factor.1, f32[4,4]{1,0:T(4,128)} %tendency.1, f32[4,128,8,512]{3,2,1,0:T(8,128)} %bitcast.13, f32[8,4,8,128]{3,2,1,0:T(8,128)} %fusion.1.obs), custom_call_target="tpu_custom_call" | custom-call | tf_op jit(solution)/shard_map/pallas_call | solution.py:430
  389.1 11.6 %copy.13 = f32[8,4,128,512]{3,2,1,0:T(8,128)} copy(f32[8,4,128,512]{3,0,2,1:T(8,128)} %bitcast.12) | data formatting | bytes 16777216 | tf_op jit(solution)/shard_map/transpose | solution.py:457
  (4 shorter events, 0.0 us)

commit v2 on v1

--- a/solution.py
+++ b/solution.py
@@ -173,14 +173,14 @@
 
 def analysis_kernel(
     groups, tiles, per_device, patch_lines, lanes_own,
-    factor, tendency, state, obs, result,
-    field, outbox, inbox, answer, obs_in, dev, centre, picked,
+    factor, tendency, state, edges, obs, result,
+    raw, field, outbox, inbox, answer, obs_in, dev, centre, picked,
     load_sem, halo_send, halo_recv, obs_send, obs_recv, obs_own,
     go_send, go_recv, go_own, back_send, back_recv, back_own,
 ):
     mine = lax.axis_index("mem")
     tile = lax.axis_index("dom")
-    variables, lines, share, span = state.shape
+    share, variables, lines, span = state.shape
     members = groups * share
     device_lines = per_device * patch_lines
     chunks = variables * patch_lines
@@ -188,8 +188,17 @@
     upper = lax.rem(tile + 1, tiles)
     lower = lax.rem(tile + tiles - 1, tiles)
 
-    load = pltpu.make_async_copy(state, field.at[:, pl.ds(1, lines)], load_sem)
-    load.start()
+    parts = 4
+    part_lines = lines // parts
+
+    def load(q):
+        rows = pl.ds(q * part_lines, part_lines)
+        return pltpu.make_async_copy(
+            state.at[:, :, rows], raw.at[:, :, rows], load_sem.at[q]
+        )
+
+    for q in range(parts):
+        load(q).start()
 
     barrier = pltpu.get_barrier_semaphore()
     for t in range(1, groups):
@@ -199,10 +208,10 @@
     pl.semaphore_wait(barrier, groups + 1)
 
     halos = []
-    for side, (line, place, other) in enumerate(((lines - 1, 0, upper), (0, lines + 1, lower))):
+    for side, (place, other) in enumerate(((0, upper), (lines + 1, lower))):
         halos.append(
             pltpu.make_async_remote_copy(
-                src_ref=state.at[:, pl.ds(line, 1)],
+                src_ref=edges.at[side],
                 dst_ref=field.at[:, pl.ds(place, 1)],
                 send_sem=halo_send.at[side],
                 recv_sem=halo_recv.at[side],
@@ -255,7 +264,17 @@
     keep = pltpu.make_async_copy(obs.at[mine], obs_in.at[mine], obs_own)
     keep.start()
 
-    load.wait()
+    for q in range(parts):
+        load(q).wait()
+
+        def turn(b, carry, q=q):
+            row = pl.multiple_of(q * part_lines + b * 8, 8)
+            for v in range(variables):
+                block = raw[:, v, pl.ds(row, 8)]
+                field[v, pl.ds(row + 1, 8)] = jnp.swapaxes(block, 0, 1)
+            return carry
+
+        lax.fori_loop(0, part_lines // 8, turn, 0)
     for copy in halos:
         copy.wait()
     for place, outside in ((0, tile == 0), (lines + 1, tile == tiles - 1)):
@@ -379,6 +398,23 @@
         return carry
 
     lax.fori_loop(0, per_device, finish, 0)
+
+
+def turn_kernel(lines_first, members_out):
+    for r in range(0, lines_first.shape[1], 8):
+        members_out[:, 0, r : r + 8] = jnp.swapaxes(lines_first[0, r : r + 8], 0, 1)
+
+
+def members_first(result):
+    variables, lines, share, span = result.shape
+    block = 32
+    return pl.pallas_call(
+        turn_kernel,
+        out_shape=jax.ShapeDtypeStruct((share, variables, lines, span), jnp.float32),
+        grid=(variables, lines // block),
+        in_specs=[pl.BlockSpec((1, block, share, span), lambda v, b: (v, b, 0, 0))],
+        out_specs=pl.BlockSpec((share, 1, block, span), lambda v, b: (0, v, b, 0)),
+    )(result)
 
 
 def fused(
@@ -423,21 +459,24 @@
     places = (slot[:, None] == jnp.arange(LANES, dtype=jnp.int32)[None]).astype(jnp.float32)
     obs = jnp.dot(spread.reshape(per_tile * 8, obs_rows), places, precision=HIGH)
     obs = obs.reshape(groups, per_device, 8, LANES)
-    state = prior_ensemble.transpose(1, 2, 0, 3)
+    edges = jnp.stack([prior_ensemble[:, :, -1], prior_ensemble[:, :, 0]])
+    edges = edges.transpose(0, 2, 1, 3)[:, :, None]
     chunks = variables * patch_lines
     slots = -(-groups // lanes_own) * LANES
     dma = pltpu.SemaphoreType.DMA
     result = pl.pallas_call(
         functools.partial(analysis_kernel, groups, tiles, per_device, patch_lines, lanes_own),
-        out_shape=jax.ShapeDtypeStruct(state.shape, jnp.float32),
+        out_shape=jax.ShapeDtypeStruct((variables, lines, share, span), jnp.float32),
         in_specs=[
             pl.BlockSpec(memory_space=pltpu.SMEM),
             pl.BlockSpec(memory_space=pltpu.SMEM),
             pl.BlockSpec(memory_space=pl.ANY),
             pl.BlockSpec(memory_space=pltpu.VMEM),
+            pl.BlockSpec(memory_space=pltpu.VMEM),
         ],
         out_specs=pl.BlockSpec(memory_space=pl.ANY),
         scratch_shapes=[
+            pltpu.VMEM((share, variables, lines, span), jnp.float32),
             pltpu.VMEM((variables, lines + 2, share, span), jnp.float32),
             pltpu.VMEM((groups, per_device, variables, patch_lines, share, span), jnp.float32),
             pltpu.VMEM((per_device, groups, variables, patch_lines, share, span), jnp.float32),
@@ -446,15 +485,15 @@
             pltpu.VMEM((chunks, members, span), jnp.float32),
             pltpu.VMEM((chunks, 8, span), jnp.float32),
             pltpu.VMEM((3 * members + 48, slots), jnp.float32),
-            dma, dma((2,)), dma((2,)), dma((groups,)), dma((groups,)), dma,
+            dma((4,)), dma((2,)), dma((2,)), dma((groups,)), dma((groups,)), dma,
             dma((per_device, groups)), dma((per_device, groups)), dma((per_device,)),
             dma((per_device, groups)), dma((per_device, groups)), dma((per_device,)),
         ],
         compiler_params=pltpu.CompilerParams(
             collective_id=0, has_side_effects=True, vmem_limit_bytes=60 * 1024 * 1024
         ),
-    )(spreading_factor, tendency_matrix, state, obs)
-    return result.transpose(2, 0, 1, 3)
+    )(spreading_factor, tendency_matrix, prior_ensemble, edges, obs)
+    return members_first(result)
 
 
 def step(prior_ensemble, *rest):
@@ -463,7 +502,7 @@
     whole_lines = PATCH % span == 0 and lines % (groups * (PATCH // span)) == 0
     obs_rows = rest[2].shape[-1]
     capacity = 2 * obs_rows * PATCH // (lines * span)
-    if share % 8 == 0 and whole_lines and tiles > 1 and groups > 1 and LANES % capacity == 0:
+    if share % 8 == 0 and whole_lines and lines % 32 == 0 and tiles > 1 and groups > 1 and LANES % capacity == 0:
         return fused(prior_ensemble, *rest)
     return shards(prior_ensemble, *rest)
 

time: 401 us -> 392 us (0.978)
  local copies, waits for them, and re-layouts: 24 us -> 2.07 us
  Pallas kernels: 372 us -> 384 us
    pallas_call x0 -> x1, Pallas kernels: none -> 12.4 us  [members_first(): pl.pallas_call(turn_kernel, out_shape=jax.ShapeDtypeStruct((share, variab...]
    transpose x1 -> x0, local copies, waits for them, and re-layouts: 11.6 us -> none  [fused(): return result.transpose(2, 0, 1, 3)]
    unnamed x1 -> x0, local copies, waits for them, and re-layouts: 11.6 us -> none
where the time goes in v2:
time: 392 us
  Pallas kernels  384 us (98%)
  other arithmetic  4.61 us (1%)
    pallas_call x1, Pallas kernels, fused(): pl.pallas_call(functools.partial(analysis_kernel, groups, tiles, per_devi...  371 us
    pallas_call x1, Pallas kernels, members_first(): pl.pallas_call(turn_kernel, out_shape=jax.ShapeDtypeStruct((share, variab...  12.4 us

profile of v2, /device:TPU:9, one launch (start us, length us, event | category | flops | bytes accessed | tf_op | source)
XLA Modules:
  0.0 391.7 jit_solution(6564807772024049116)
XLA Ops:
  0.0 1.0 convert_reduce_fusion
  1.0 0.7 convert_element_type.8
  1.7 0.8 select_reduce_fusion
  2.5 0.7 mul.7
  3.2 0.7 stack.13
  3.9 0.8 broadcast_compare_fusion
  4.7 1.2 fusion.1.obs
  5.8 1.3 fusion.10
  7.2 0.7 maximum_bitcast_fusion.edges
  7.9 371.4 %shard_map.91.lines_first = f32[4,128,8,512]{3,2,1,0:T(8,128)} custom-call(f32[4]{0:T(128)} %factor.1, f32[4,4]{1,0:T(4,128)} %tendency.1, f32[8,4,128,512]{3,2,1,0:T(8,128)} %state.1, f32[2,4,1,8,512]{4,3,2,1,0:T(8,128)} %maximum_bitcast_fusion.edges, f32[8,4,8,128]{3,2,1,0:T(8,128)} %fusion.1.obs), custom_call_target="tpu_custom_call" | custom-call | tf_op jit(solution)/shard_map/pallas_call | solution.py:467
  379.3 12.4 %shard_map.92 = f32[8,4,128,512]{3,2,1,0:T(8,128)} custom-call(f32[4,128,8,512]{3,2,1,0:T(8,128)} %shard_map.91.lines_first), custom_call_target="tpu_custom_call" | custom-call | tf_op jit(solution)/shard_map/pallas_call | solution.py:411
  (5 shorter events, 0.1 us)

commit v3 on v2

--- a/solution.py
+++ b/solution.py
@@ -173,7 +173,7 @@
 
 def analysis_kernel(
     groups, tiles, per_device, patch_lines, lanes_own,
-    factor, tendency, state, edges, obs, result,
+    factor, tendency, state, obs, result,
     raw, field, outbox, inbox, answer, obs_in, dev, centre, picked,
     load_sem, halo_send, halo_recv, obs_send, obs_recv, obs_own,
     go_send, go_recv, go_own, back_send, back_recv, back_own,
@@ -197,7 +197,8 @@
             state.at[:, :, rows], raw.at[:, :, rows], load_sem.at[q]
         )
 
-    for q in range(parts):
+    turns = (0, parts - 1) + tuple(range(1, parts - 1))
+    for q in turns:
         load(q).start()
 
     barrier = pltpu.get_barrier_semaphore()
@@ -208,17 +209,16 @@
     pl.semaphore_wait(barrier, groups + 1)
 
     halos = []
-    for side, (place, other) in enumerate(((0, upper), (lines + 1, lower))):
+    for side, (line, place, other) in enumerate(((lines, 0, upper), (1, lines + 1, lower))):
         halos.append(
             pltpu.make_async_remote_copy(
-                src_ref=edges.at[side],
+                src_ref=field.at[:, pl.ds(line, 1)],
                 dst_ref=field.at[:, pl.ds(place, 1)],
                 send_sem=halo_send.at[side],
                 recv_sem=halo_recv.at[side],
                 device_id={"dom": other},
             )
         )
-        halos[-1].start()
 
     def obs_copy(t):
         to = lax.rem(mine + t, groups)
@@ -264,7 +264,7 @@
     keep = pltpu.make_async_copy(obs.at[mine], obs_in.at[mine], obs_own)
     keep.start()
 
-    for q in range(parts):
+    for q in turns:
         load(q).wait()
 
         def turn(b, carry, q=q):
@@ -275,6 +275,9 @@
             return carry
 
         lax.fori_loop(0, part_lines // 8, turn, 0)
+        if q == parts - 1:
+            for copy in halos:
+                copy.start()
     for copy in halos:
         copy.wait()
     for place, outside in ((0, tile == 0), (lines + 1, tile == tiles - 1)):
@@ -407,7 +410,7 @@
 
 def members_first(result):
     variables, lines, share, span = result.shape
-    block = 32
+    block = 64 if lines % 64 == 0 else 32
     return pl.pallas_call(
         turn_kernel,
         out_shape=jax.ShapeDtypeStruct((share, variables, lines, span), jnp.float32),
@@ -459,8 +462,6 @@
     places = (slot[:, None] == jnp.arange(LANES, dtype=jnp.int32)[None]).astype(jnp.float32)
     obs = jnp.dot(spread.reshape(per_tile * 8, obs_rows), places, precision=HIGH)
     obs = obs.reshape(groups, per_device, 8, LANES)
-    edges = jnp.stack([prior_ensemble[:, :, -1], prior_ensemble[:, :, 0]])
-    edges = edges.transpose(0, 2, 1, 3)[:, :, None]
     chunks = variables * patch_lines
     slots = -(-groups // lanes_own) * LANES
     dma = pltpu.SemaphoreType.DMA
@@ -471,7 +472,6 @@
             pl.BlockSpec(memory_space=pltpu.SMEM),
             pl.BlockSpec(memory_space=pltpu.SMEM),
             pl.BlockSpec(memory_space=pl.ANY),
-            pl.BlockSpec(memory_space=pltpu.VMEM),
             pl.BlockSpec(memory_space=pltpu.VMEM),
         ],
         out_specs=pl.BlockSpec(memory_space=pl.ANY),
@@ -492,7 +492,7 @@
         compiler_params=pltpu.CompilerParams(
             collective_id=0, has_side_effects=True, vmem_limit_bytes=60 * 1024 * 1024
         ),
-    )(spreading_factor, tendency_matrix, prior_ensemble, edges, obs)
+    )(spreading_factor, tendency_matrix, prior_ensemble, obs)
     return members_first(result)
 
 

time: 392 us -> 388 us (0.990)
  no operation moved by 1% of the time
where the time goes in v3:
time: 388 us; the launch traced here: 387 us
  Pallas kernels  381 us (98%)
  other arithmetic  3.95 us (1%)
    pallas_call x1, Pallas kernels, fused(): pl.pallas_call(functools.partial(analysis_kernel, groups, tiles, per_devi...  372 us
    pallas_call x1, Pallas kernels, members_first(): pl.pallas_call(turn_kernel, out_shape=jax.ShapeDtypeStruct((share, variab...  9.38 us

profile of v3, /device:TPU:9, one launch (start us, length us, event | category | flops | bytes accessed | tf_op | source)
XLA Modules:
  0.0 387.3 jit_solution(7555193343858185660)
XLA Ops:
  0.0 1.0 convert_reduce_fusion
  1.0 0.7 convert_element_type.8
  1.7 0.8 select_reduce_fusion
  2.5 0.7 mul.7
  3.2 0.7 stack.9
  3.9 0.8 broadcast_compare_fusion
  4.7 1.2 fusion.1.obs
  5.8 372.1 %shard_map.91.lines_first = f32[4,128,8,512]{3,2,1,0:T(8,128)} custom-call(f32[4]{0:T(128)} %factor.1, f32[4,4]{1,0:T(4,128)} %tendency.1, f32[8,4,128,512]{3,2,1,0:T(8,128)} %state.1, f32[8,4,8,128]{3,2,1,0:T(8,128)} %fusion.1.obs), custom_call_target="tpu_custom_call" | custom-call | tf_op jit(solution)/shard_map/pallas_call | solution.py:468
  377.9 9.4 %shard_map.92 = f32[8,4,128,512]{3,2,1,0:T(8,128)} custom-call(f32[4,128,8,512]{3,2,1,0:T(8,128)} %shard_map.91.lines_first), custom_call_target="tpu_custom_call" | custom-call | tf_op jit(solution)/shard_map/pallas_call | solution.py:414
  (4 shorter events, 0.0 us)
